TPU v7x, 32 devices: a whole 2x2x4 slice. The times are simulated.
32 devices in a mesh: seg: 4 (over z), mpo: 4 (over x, core), sec: 2 (over y).
Axes of the slice: x: 2, y: 2, z: 4, core: 2. Of those that a mesh axis runs over, the one named last changes fastest.
Arguments:
- state: bfloat16 [4, 1024, 1024], P('seg', 'sec'), may hold values from -6 to 6
- left_env: bfloat16 [4, 12, 1024, 1024], P('seg', 'mpo', 'sec'), may hold values from -0.1875 to 0.1875
- right_env: bfloat16 [4, 12, 1024, 1024], P('seg', 'mpo'), may hold values from -0.1875 to 0.1875
- inv_singular: float32 [4, 1024], P('seg'), may hold values from 0.5 to 2
- sketch_cols: bfloat16 [4, 2, 1024, 256], P('seg'), may hold values from -6 to 6
- kept_ranks: int32 [4], P('seg'), may hold values from 128 to 256, as said below
Outputs:
- final_state: bfloat16 [4, 1024, 1024], P('seg', 'sec')
Inputs may be any that keep to these rules, and one draw needn't show every extreme that they name: `kept_ranks`: each segment keeps between 128 and 256 ranks; some segment keeps exactly 256.
All inputs are finite; a program needn't handle non-finite values.
Results may differ from a plain program's by a relative error of at most 0.025.
Values may be sent and summed in bfloat16 or wider, within the bound.
No kernel may reach another device: no remote copies, remote signals or barrier semaphores. Data moves between devices by JAX's collectives and lax.ppermute only.
A program may use at most 128 MiB of HBM per device.

v0:
```python
import jax
import jax.numpy as jnp
from jax import lax
from jax.sharding import PartitionSpec as P

ITERS = 2
TAU = 0.3
MOMENTUM = 0.5
EPS = 1e-06


def from_behind(block, axis, distance):
    devices = range(lax.axis_size(axis))
    route = [(i - distance, i) for i in devices if i - distance in devices]
    return lax.ppermute(block, axis, route)


def left_products(left, rows):
    return jnp.einsum(
        "kij,jn->kin",
        left,
        lax.all_gather(rows, "sec", axis=0, tiled=True),
        preferred_element_type=jnp.float32,
    )


def gradient_step(rows, previous, left, right):
    width = rows.shape[1]
    first = left_products(left, rows).astype(jnp.bfloat16)
    partial_sum = jnp.einsum("kij,kjn->in", first, right, preferred_element_type=jnp.float32)
    total = lax.psum(partial_sum, "mpo")
    shifted = rows.astype(jnp.float32) - TAU * total
    if previous is not None:
        shifted = shifted - MOMENTUM * previous.astype(jnp.float32)
    squares = lax.psum(jnp.sum(shifted * shifted), "sec")
    return (shifted * (width * lax.rsqrt(squares + EPS))).astype(jnp.bfloat16)


def run_steps(start_rows, left, right):
    current = start_rows
    previous = None
    for step in range(ITERS):
        current, previous = (gradient_step(current, previous, left, right), current)
    return current


def truncate(rows, omega, rank):
    columns = omega.shape[1]
    sketch = jnp.dot(rows, omega, preferred_element_type=jnp.float32)
    keep = (jnp.arange(columns) < rank).astype(jnp.float32)
    as_float = rows.astype(jnp.float32)
    gram, cross = lax.psum(
        (
            jnp.dot(sketch.T, sketch, precision=lax.Precision.HIGHEST),
            jnp.dot(sketch.T, as_float, precision=lax.Precision.HIGHEST),
        ),
        "sec",
    )
    factor = jnp.linalg.cholesky(gram)
    basis = (
        lax.linalg.triangular_solve(factor, sketch.T, left_side=True, lower=True).T * keep[None, :]
    )
    coeffs = lax.linalg.triangular_solve(factor, cross, left_side=True, lower=True) * keep[:, None]
    return jnp.dot(basis, coeffs, precision=lax.Precision.HIGHEST).astype(jnp.bfloat16)


def on_device(state, left_env, right_env, inv_singular, sketch_cols, kept_ranks):
    rows = state[0]
    left = left_env[0]
    right = right_env[0]
    scales = inv_singular[0]
    rank = kept_ranks[0]
    width = rows.shape[1]
    neighbour = from_behind(rows, "seg", 1)
    merged = (rows.astype(jnp.float32) + neighbour.astype(jnp.float32) * scales[None, :]).astype(
        jnp.bfloat16
    )
    current = run_steps(merged, left, right)
    middle = truncate(current, sketch_cols[0, 0], rank)
    expanded = left_products(left, middle).astype(jnp.bfloat16)
    summed = lax.psum_scatter(
        jnp.einsum("ia,kin->akn", middle, expanded, preferred_element_type=jnp.float32),
        "sec",
        scatter_dimension=0,
        tiled=True,
    )
    message = (summed * (1.0 / width)).astype(jnp.bfloat16)
    arrived = from_behind(message, "seg", 1)
    left_next = (
        left.astype(jnp.float32) + jnp.transpose(arrived.astype(jnp.float32), (1, 0, 2))
    ).astype(jnp.bfloat16)
    neighbour_two = from_behind(middle, "seg", -1)
    merged_two = (
        middle.astype(jnp.float32) + neighbour_two.astype(jnp.float32) * scales[None, :]
    ).astype(jnp.bfloat16)
    current = run_steps(merged_two, left_next, right)
    final_rows = truncate(current, sketch_cols[0, 1], rank)
    return final_rows[None]


def solution(mesh):
    return jax.shard_map(
        on_device,
        mesh=mesh,
        in_specs=(
            P("seg", "sec", None),
            P("seg", "mpo", "sec", None),
            P("seg", "mpo", None, None),
            P("seg", None),
            P("seg", None, None, None),
            P("seg"),
        ),
        out_specs=P("seg", "sec", None),
        check_vma=False,
    )
```

profile of v0, /device:TPU:0, one launch (start us, length us, event | category | flops | bytes accessed | tf_op | source)
XLA Modules:
  0.0 956.5 jit_solution(16439634779600430897)
XLA Ops:
  6.5 5.0 collective-permute-start
  11.5 22.6 %collective-permute-done = bf16[512,1024]{1,0:T(8,128)(2,1)S(1)} collective-permute-done((bf16[512,1024]{1,0:T(8,128)(2,1)}, bf16[512,1024]{1,0:T(8,128)(2,1)S(1)}, u32[]{:S(2)}, u32[]{:S(2)}) %collective-permute-start) | collective-permute-done | bytes 1048608 | tf_op jit(solution)/shard_map/ppermute | solution.py:15
  34.2 2.7 add_convert_fusion.1
  36.9 35.3 %all-gather.6.cloned.1.call-done = bf16[1024,1024]{1,0:T(8,128)(2,1)} async-done(((bf16[512,1024]{1,0:T(8,128)(2,1)}), bf16[1024,1024]{1,0:T(8,128)(2,1)}) %all-gather.6.cloned.1.call-update) | async-done | bytes 2097168 | tf_op jit(solution)/shard_map/all_gather | solution.py:22
  72.2 5.2 fusion.17
  77.4 7.5 fusion.33
  85.1 51.5 %all-reduce.10.cloned.1.call-done = f32[512,1024]{1,0:T(8,128)} async-done(((f32[512,1024]{1,0:T(8,128)}), f32[512,1024]{1,0:T(8,128)}) %all-reduce.10.cloned.1.call-update) | async-done | bytes 2097168 | tf_op jit(solution)/shard_map/psum | solution.py:31
  136.5 2.9 multiply_reduce_fusion.3
  139.4 5.5 psum.85
  145.7 1.3 multiply_convert_fusion.4
  147.3 33.1 %all-gather.8.cloned.1.call-done = bf16[1024,1024]{1,0:T(8,128)(2,1)} async-done(((bf16[512,1024]{1,0:T(8,128)(2,1)}), bf16[1024,1024]{1,0:T(8,128)(2,1)}) %all-gather.8.cloned.1.call-update) | async-done | bytes 2097168 | tf_op jit(solution)/shard_map/all_gather | solution.py:22
  180.4 5.9 fusion.15
  186.4 7.5 fusion.38
  194.0 51.5 %all-reduce.12.cloned.1.call-done = f32[512,1024]{1,0:T(8,128)} async-done(((f32[512,1024]{1,0:T(8,128)}), f32[512,1024]{1,0:T(8,128)}) %all-reduce.12.cloned.1.call-update) | async-done | bytes 2097168 | tf_op jit(solution)/shard_map/psum | solution.py:31
  245.5 2.8 multiply_reduce_fusion.2
  248.2 5.5 psum.87
  254.5 2.3 multiply_convert_fusion.3
  257.2 2.0 fusion.116
  259.2 1.7 fusion.115
  261.9 45.3 %all-reduce.20.cloned.1.call-done = (f32[256,1024]{1,0:T(8,128)}, f32[256,256]{0,1:T(8,128)}) async-done(((f32[256,1024]{1,0:T(8,128)}, f32[256,256]{0,1:T(8,128)}), (f32[256,1024]{1,0:T(8,128)}, f32[256,256]{0,1:T(8,128)})) %all-reduce.20.cloned.1.call-update) | async-done | bytes 1310736 | tf_op jit(solution)/shard_map/psum | solution.py:52
  307.1 1.1 copy.8
  309.2 11.7 %cholesky.130 = f32[128,128]{1,0:T(8,128)S(1)} custom-call(f32[128,128]{1,0:T(8,128)S(1)} %cholesky.194), custom_call_target="Cholesky" | custom-call | tf_op jit(solution)/shard_map/jit(cholesky)/cholesky | solution.py:59
  321.0 9.8 %custom-call.17 = f32[1,128,128]{1,2,0:T(8,128)S(1)} custom-call(f32[1,128,128]{2,1,0:T(8,128)S(1)} %get-tuple-element.71), custom_call_target="InvertDiagBlocksLowerTriangular" | custom-call | tf_op jit(solution)/shard_map/jit(cholesky)/cholesky | solution.py:59
  331.3 11.7 %cholesky.147 = f32[128,128]{1,0:T(8,128)S(1)} custom-call(f32[128,128]{1,0:T(8,128)S(1)} %convolution_subtract_fusion.5), custom_call_target="Cholesky" | custom-call | tf_op jit(solution)/shard_map/jit(cholesky)/cholesky | solution.py:59
  345.2 4.5 while.8
  346.3 1.4 bitcast_dynamic-update-slice_fusion.4
  348.3 1.4 bitcast_dynamic-update-slice_fusion.4
  349.8 19.7 %custom-call.18 = f32[2,128,128]{1,2,0:T(8,128)S(1)} custom-call(f32[2,128,128]{2,1,0:T(8,128)S(1)} %get-tuple-element.36), custom_call_target="InvertDiagBlocksLowerTriangular" | custom-call | tf_op jit(solution)/shard_map/triangular_solve/custom-call.0 | solution.py:61
  372.8 3.0 convolution_convert_fusion.1
  375.9 33.2 %all-gather.10.cloned.1.call-done = bf16[1024,1024]{1,0:T(8,128)(2,1)} async-done(((bf16[512,1024]{1,0:T(8,128)(2,1)}), bf16[1024,1024]{1,0:T(8,128)(2,1)}) %all-gather.10.cloned.1.call-update) | async-done | bytes 2097168 | tf_op jit(solution)/shard_map/all_gather | solution.py:22
  409.1 11.1 %fusion.9 = f32[1024,3,1024]{2,0,1:T(8,128)} fusion(bf16[1,3,512,1024]{3,2,1,0:T(8,128)(2,1)S(1)} %copy-done.11, bf16[1024,1024]{1,0:T(8,128)(2,1)} %all-gather.10.cloned.1.call-done, bf16[512,1024]{1,0:T(8,128)(2,1)} %convolution_convert_fusion.1), kind=kOutput, calls=%fused_computation.15 | convolution fusion | flops 6444023808 | bytes 18874368 | tf_op jit(solution)/shard_map/ia,kin->akn/dot_general | solution.py:82
  420.3 1.1 copy-done.4
  421.4 1.3 collective-permute-start.1
  422.7 142.1 %reduce-scatter.2.cloned.1.call-done = f32[512,3,1024]{2,0,1:T(8,128)} async-done(((f32[1024,3,1024]{2,0,1:T(8,128)}), f32[512,3,1024]{2,0,1:T(8,128)}) %reduce-scatter.2.cloned.1.call-update) | async-done | bytes 6291472 | tf_op jit(solution)/shard_map/reduce_scatter | solution.py:81
  564.8 5.4 multiply_convert_fusion
  570.2 5.1 collective-permute-start.2
  575.3 1.4 add_convert_fusion
  576.9 30.5 %all-gather.12.cloned.1.call-done = bf16[1024,1024]{1,0:T(8,128)(2,1)} async-done(((bf16[512,1024]{1,0:T(8,128)(2,1)}), bf16[1024,1024]{1,0:T(8,128)(2,1)}) %all-gather.12.cloned.1.call-update) | async-done | bytes 2097168 | tf_op jit(solution)/shard_map/all_gather | solution.py:22
  607.4 33.9 %collective-permute-done.2 = bf16[512,3,1024]{2,0,1:T(8,128)(2,1)} collective-permute-done((bf16[512,3,1024]{2,0,1:T(8,128)(2,1)}, bf16[512,3,1024]{2,0,1:T(8,128)(2,1)}, u32[]{:S(2)}, u32[]{:S(2)}) %collective-permute-start.2) | collective-permute-done | bytes 3145760 | tf_op jit(solution)/shard_map/ppermute | solution.py:15
  641.3 6.9 fusion.28
  648.2 7.6 fusion.43
  655.9 52.5 %all-reduce.14.cloned.1.call-done = f32[512,1024]{1,0:T(8,128)} async-done(((f32[512,1024]{1,0:T(8,128)}), f32[512,1024]{1,0:T(8,128)}) %all-reduce.14.cloned.1.call-update) | async-done | bytes 2097168 | tf_op jit(solution)/shard_map/psum | solution.py:31
  708.4 2.9 multiply_reduce_fusion.1
  711.3 5.5 psum.91
  717.5 1.3 multiply_convert_fusion.2
  718.9 33.3 %all-gather.14.cloned.1.call-done = bf16[1024,1024]{1,0:T(8,128)(2,1)} async-done(((bf16[512,1024]{1,0:T(8,128)(2,1)}), bf16[1024,1024]{1,0:T(8,128)(2,1)}) %all-gather.14.cloned.1.call-update) | async-done | bytes 2097168 | tf_op jit(solution)/shard_map/all_gather | solution.py:22
  752.3 6.9 fusion.26
  759.2 7.5 fusion.48
  766.8 51.5 %all-reduce.16.cloned.1.call-done = f32[512,1024]{1,0:T(8,128)} async-done(((f32[512,1024]{1,0:T(8,128)}), f32[512,1024]{1,0:T(8,128)}) %all-reduce.16.cloned.1.call-update) | async-done | bytes 2097168 | tf_op jit(solution)/shard_map/psum | solution.py:31
  818.3 2.8 multiply_reduce_fusion
  821.0 5.8 psum.93
  827.5 2.3 multiply_convert_fusion.1
  830.2 2.0 fusion.118
  832.2 1.7 fusion.117
  834.0 46.2 %all-reduce.18.cloned.1.call-done = (f32[256,1024]{1,0:T(8,128)}, f32[256,256]{0,1:T(8,128)}) async-done(((f32[256,1024]{1,0:T(8,128)}, f32[256,256]{0,1:T(8,128)}), (f32[256,1024]{1,0:T(8,128)}, f32[256,256]{0,1:T(8,128)})) %all-reduce.18.cloned.1.call-update) | async-done | bytes 1310736 | tf_op jit(solution)/shard_map/psum | solution.py:52
  880.2 1.1 copy.11
  882.2 11.7 %cholesky.164 = f32[128,128]{1,0:T(8,128)S(1)} custom-call(f32[128,128]{1,0:T(8,128)S(1)} %cholesky.197), custom_call_target="Cholesky" | custom-call | tf_op jit(solution)/shard_map/jit(cholesky)/cholesky | solution.py:59
  894.0 9.8 %custom-call.20 = f32[1,128,128]{1,2,0:T(8,128)S(1)} custom-call(f32[1,128,128]{2,1,0:T(8,128)S(1)} %get-tuple-element.67), custom_call_target="InvertDiagBlocksLowerTriangular" | custom-call | tf_op jit(solution)/shard_map/jit(cholesky)/cholesky | solution.py:59
  904.3 11.9 %cholesky.181 = f32[128,128]{1,0:T(8,128)S(1)} custom-call(f32[128,128]{1,0:T(8,128)S(1)} %convolution_subtract_fusion.4), custom_call_target="Cholesky" | custom-call | tf_op jit(solution)/shard_map/jit(cholesky)/cholesky | solution.py:59
  919.0 4.1 while.9
  919.7 1.4 bitcast_dynamic-update-slice_fusion.5
  921.7 1.4 bitcast_dynamic-update-slice_fusion.5
  923.2 19.7 %custom-call.21 = f32[2,128,128]{1,2,0:T(8,128)S(1)} custom-call(f32[2,128,128]{2,1,0:T(8,128)S(1)} %get-tuple-element.38), custom_call_target="InvertDiagBlocksLowerTriangular" | custom-call | tf_op jit(solution)/shard_map/triangular_solve/custom-call.0 | solution.py:61
  946.2 3.0 fusion.53
  (98 shorter events, 16.5 us)
Async XLA Ops:
  6.5 65.7 %all-gather.6.cloned.1.call-start = ((), (), s32[]{:S(2)}) async-start(), calls=%async_computation.1 | async-start | bytes 3145728 | tf_op jit(solution)/shard_map/all_gather | solution.py:22
  6.5 27.6 %collective-permute-start = (bf16[512,1024]{1,0:T(8,128)(2,1)}, bf16[512,1024]{1,0:T(8,128)(2,1)S(1)}, u32[]{:S(2)}, u32[]{:S(2)}) collective-permute-start(bf16[512,1024]{1,0:T(8,128)(2,1)} %bitcast.191), channel_id=1, source_target_pairs={{0,8},{8,16},{16,24},{1,9},{9,17},{17,25},{2,10},{10,18},{18,26},{... | collective-permute-start | bytes 3145736 | tf_op jit(solution)/shard_map/ppermute | solution.py:15
  34.2 38.0 %copy-start.10 = (bf16[1,3,512,1024]{3,2,1,0:T(8,128)(2,1)S(1)}, bf16[1,3,512,1024]{3,2,1,0:T(8,128)(2,1)}, u32[]{:S(2)}) copy-start(bf16[1,3,512,1024]{3,2,1,0:T(8,128)(2,1)} %param.12) | copy-start | bytes 9437188
  36.9 99.6 %all-reduce.10.cloned.1.call-start = ((), (), s32[]{:S(2)}) async-start(), calls=%async_computation.2 | async-start | bytes 4194304 | tf_op jit(solution)/shard_map/psum | solution.py:31
  85.0 51.6 %copy-start.1 = (bf16[512,1024]{1,0:T(8,128)(2,1)S(1)}, bf16[512,1024]{1,0:T(8,128)(2,1)}, u32[]{:S(2)}) copy-start(bf16[512,1024]{1,0:T(8,128)(2,1)} %add_convert_fusion.1) | copy-start | bytes 3145732
  85.0 95.4 %all-gather.8.cloned.1.call-start = ((), (), s32[]{:S(2)}) async-start(), calls=%async_computation.3 | async-start | bytes 3145728 | tf_op jit(solution)/shard_map/all_gather | solution.py:22
  136.5 9.1 copy-start.5
  147.1 98.4 %all-reduce.12.cloned.1.call-start = ((), (), s32[]{:S(2)}) async-start(), calls=%async_computation.4 | async-start | bytes 4194304 | tf_op jit(solution)/shard_map/psum | solution.py:31
  193.9 51.6 %copy-start.3 = (bf16[512,1024]{1,0:T(8,128)(2,1)S(1)}, bf16[512,1024]{1,0:T(8,128)(2,1)}, u32[]{:S(2)}) copy-start(bf16[512,1024]{1,0:T(8,128)(2,1)} %multiply_convert_fusion.4) | copy-start | bytes 3145732
  193.9 113.2 %all-reduce.20.cloned.1.call-start = ((), (), s32[]{:S(2)}) async-start(), calls=%async_computation.12 | async-start | bytes 2621440 | tf_op jit(solution)/shard_map/psum | solution.py:52
  254.5 2.3 copy-start.12
  261.0 148.1 %all-gather.10.cloned.1.call-start = ((), (), s32[]{:S(2)}) async-start(), calls=%async_computation.5 | async-start | bytes 3145728 | tf_op jit(solution)/shard_map/all_gather | solution.py:22
  330.8 40.1 %copy-start.7 = (f32[256,1024]{1,0:T(8,128)S(1)}, f32[256,1024]{1,0:T(8,128)}, u32[]{:S(2)}) copy-start(f32[256,1024]{1,0:T(8,128)} %get-tuple-element.58) | copy-start | bytes 3145732
  372.8 36.3 %copy-start.11 = (bf16[1,3,512,1024]{3,2,1,0:T(8,128)(2,1)S(1)}, bf16[1,3,512,1024]{3,2,1,0:T(8,128)(2,1)}, u32[]{:S(2)}) copy-start(bf16[1,3,512,1024]{3,2,1,0:T(8,128)(2,1)} %param.12) | copy-start | bytes 9437188
  375.8 189.0 %reduce-scatter.2.cloned.1.call-start = ((), (), s32[]{:S(2)}) async-start(), calls=%async_computation.6 | async-start | bytes 18874368 | tf_op jit(solution)/shard_map/reduce_scatter | solution.py:81
  420.2 1.2 copy-start.4
  420.2 155.1 %copy-start.9 = (f32[1,1024]{1,0:T(1,128)S(1)}, f32[1,1024]{1,0:T(1,128)}, u32[]{:S(2)}) copy-start(f32[1,1024]{1,0:T(1,128)} %param.14) | copy-start | bytes 12292
  420.2 187.2 %all-gather.12.cloned.1.call-start = ((), (), s32[]{:S(2)}) async-start(), calls=%async_computation.7 | async-start | bytes 3145728 | tf_op jit(solution)/shard_map/all_gather | solution.py:22
  421.4 153.9 %collective-permute-start.1 = (bf16[512,1024]{1,0:T(8,128)(2,1)S(1)}, bf16[512,1024]{1,0:T(8,128)(2,1)S(1)}, u32[]{:S(2)}, u32[]{:S(2)}) collective-permute-start(bf16[512,1024]{1,0:T(8,128)(2,1)S(1)} %copy-done.4), channel_id=1, source_target_pairs={{8,0},{16,8},{24,16},{9,1},{17,9},{25,17},{10,2},{18,10},{26,18},{... | collective-permute-start | bytes 3145736 | tf_op jit(solution)/shard_map/ppermute | solution.py:15
  570.2 71.0 %collective-permute-start.2 = (bf16[512,3,1024]{2,0,1:T(8,128)(2,1)}, bf16[512,3,1024]{2,0,1:T(8,128)(2,1)}, u32[]{:S(2)}, u32[]{:S(2)}) collective-permute-start(bf16[512,3,1024]{2,0,1:T(8,128)(2,1)} %multiply_convert_fusion), channel_id=1, source_target_pairs={{0,8},{8,16},{16,24},{1,9},{9,17},{17,25},{2,10},{10,18},{18,26},{... | collective-permute-start | bytes 9437192 | tf_op jit(solution)/shard_map/ppermute | solution.py:15
  576.7 131.7 %all-reduce.14.cloned.1.call-start = ((), (), s32[]{:S(2)}) async-start(), calls=%async_computation.8 | async-start | bytes 4194304 | tf_op jit(solution)/shard_map/psum | solution.py:31
  655.8 52.6 %copy-start = (bf16[512,1024]{1,0:T(8,128)(2,1)S(1)}, bf16[512,1024]{1,0:T(8,128)(2,1)}, u32[]{:S(2)}) copy-start(bf16[512,1024]{1,0:T(8,128)(2,1)} %add_convert_fusion) | copy-start | bytes 3145732
  655.8 96.4 %all-gather.14.cloned.1.call-start = ((), (), s32[]{:S(2)}) async-start(), calls=%async_computation.9 | async-start | bytes 3145728 | tf_op jit(solution)/shard_map/all_gather | solution.py:22
  708.4 9.1 copy-start.6
  718.9 99.4 %all-reduce.16.cloned.1.call-start = ((), (), s32[]{:S(2)}) async-start(), calls=%async_computation.10 | async-start | bytes 4194304 | tf_op jit(solution)/shard_map/psum | solution.py:31
  766.7 51.6 %copy-start.2 = (bf16[512,1024]{1,0:T(8,128)(2,1)S(1)}, bf16[512,1024]{1,0:T(8,128)(2,1)}, u32[]{:S(2)}) copy-start(bf16[512,1024]{1,0:T(8,128)(2,1)} %multiply_convert_fusion.2) | copy-start | bytes 3145732
  766.7 113.4 %all-reduce.18.cloned.1.call-start = ((), (), s32[]{:S(2)}) async-start(), calls=%async_computation.11 | async-start | bytes 2621440 | tf_op jit(solution)/shard_map/psum | solution.py:52
  827.5 2.3 copy-start.13
  903.8 40.5 %copy-start.8 = (f32[256,1024]{1,0:T(8,128)S(1)}, f32[256,1024]{1,0:T(8,128)}, u32[]{:S(2)}) copy-start(f32[256,1024]{1,0:T(8,128)} %get-tuple-element.56) | copy-start | bytes 3145732
Sparse Core Ops, SparseCore 0:
  37.0 35.1 all-gather.5
  85.1 51.3 all-reduce.9
  147.2 33.1 all-gather.7
  194.0 51.3 all-reduce.11
  261.1 46.0 all-reduce.19
  375.9 33.0 all-gather.9
  420.3 144.4 reduce-scatter.1
  576.8 30.5 all-gather.11
  655.9 52.3 all-reduce.13
  719.0 33.1 all-gather.13
  766.8 51.3 all-reduce.15
  834.1 46.0 all-reduce.17
where the time goes:
time: 962 us; the launch traced here: 956 us
  waiting for transfers between devices  663 us (69%)
  other arithmetic  138 us (14%)
  matrix products  88.1 us (9%)
  blocking collectives  22.4 us (2%)
  between operations  20.6 us (2%)
  starting transfers between devices  12.3 us (1%)
  local copies, waits for them, and re-layouts  11.6 us (1%)
    psum x4, waiting for transfers between devices, gradient_step(): total = lax.psum(partial_sum, 'mpo')  207 us
    all_gather x5, waiting for transfers between devices, left_products(): lax.all_gather(rows, 'sec', axis=0, tiled=True)  165 us
    reduce_scatter x1, waiting for transfers between devices, on_device(): lax.psum_scatter(jnp.einsum('ia,kin->akn', middle, expanded, preferred_el...  142 us
    psum x2, waiting for transfers between devices, truncate(): lax.psum((jnp.dot(sketch.T, sketch, precision=lax.Precision.HIGHEST), jnp...  91.4 us
    another operation x13, other arithmetic, truncate(): factor = jnp.linalg.cholesky(gram)  68.9 us
    ppermute x3, waiting for transfers between devices, from_behind(): return lax.ppermute(block, axis, route)  56.5 us
    another operation x5, other arithmetic, truncate(): lax.linalg.triangular_solve(factor, sketch.T, left_side=True, lower=True)  39.4 us
    dot_general x4, matrix products, gradient_step(): jnp.einsum('kij,kjn->in', first, right, preferred_element_type=jnp.float32)  30.2 us
  transfers between devices with their start and end apart: 15, of which 14 were waited for; matrix products, arithmetic and copies ran while one was open for 1% of the time, Pallas kernels for 0%

commit v1 on v0

--- a/solution.py
+++ b/solution.py
@@ -9,6 +9,18 @@
 EPS = 1e-06
 
 
+def doubled_up(shard, axis, dim):
+    ways, here, step = (lax.axis_size(axis), lax.axis_index(axis), shard.shape[dim])
+    line, have = (shard, 1)
+    while have < ways:
+        line = jnp.concatenate(
+            [line, lax.ppermute(line, axis, [(d, (d - have) % ways) for d in range(ways)])],
+            axis=dim,
+        )
+        have = 2 * have
+    return jnp.roll(line, here * step, axis=dim)
+
+
 def from_behind(block, axis, distance):
     devices = range(lax.axis_size(axis))
     route = [(i - distance, i) for i in devices if i - distance in devices]
@@ -17,10 +29,7 @@
 
 def left_products(left, rows):
     return jnp.einsum(
-        "kij,jn->kin",
-        left,
-        lax.all_gather(rows, "sec", axis=0, tiled=True),
-        preferred_element_type=jnp.float32,
+        "kij,jn->kin", left, doubled_up(rows, "sec", 0), preferred_element_type=jnp.float32
     )
 
 

time: 962 us -> 920 us (0.956)
  waiting for transfers between devices: 663 us -> 623 us
    all_gather x5 -> x0, waiting for transfers between devices: 165 us -> none  [left_products(): lax.all_gather(rows, 'sec', axis=0, tiled=True)]
    ppermute x0 -> x5, waiting for transfers between devices: none -> 115 us  [doubled_up(): lax.ppermute(line, axis, [(d, (d - have) % ways) for d in range(ways)])]
    dot_general x4, matrix products: 30.2 us -> 51.7 us  [gradient_step(): jnp.einsum('kij,kjn->in', first, right, preferred_element_type=jnp.float32)]
    dot_general x4 -> x1, matrix products: 24.9 us -> 4.88 us  [left_products(): jnp.einsum('kij,jn->kin', left, doubled_up(rows, 'sec', 0), preferred_ele...]
  transfers between devices with their start and end apart: 15 -> 15, of which waited for: 14 -> 15; matrix products, arithmetic and copies ran while one was open for 1% -> 0% of each run, Pallas kernels for 0% -> 0%
where the time goes in v1:
time: 920 us; the launch traced here: 914 us
  waiting for transfers between devices  623 us (68%)
  other arithmetic  135 us (15%)
  matrix products  83.9 us (9%)
  blocking collectives  22.6 us (2%)
  between operations  20.4 us (2%)
  starting transfers between devices  17.7 us (2%)
  local copies, waits for them, and re-layouts  10.6 us (1%)
    psum x4, waiting for transfers between devices, gradient_step(): total = lax.psum(partial_sum, 'mpo')  210 us
    reduce_scatter x1, waiting for transfers between devices, on_device(): lax.psum_scatter(jnp.einsum('ia,kin->akn', middle, expanded, preferred_el...  144 us
    ppermute x5, waiting for transfers between devices, doubled_up(): lax.ppermute(line, axis, [(d, (d - have) % ways) for d in range(ways)])  115 us
    psum x2, waiting for transfers between devices, truncate(): lax.psum((jnp.dot(sketch.T, sketch, precision=lax.Precision.HIGHEST), jnp...  91.4 us
    another operation x13, other arithmetic, truncate(): factor = jnp.linalg.cholesky(gram)  68.9 us
    ppermute x3, waiting for transfers between devices, from_behind(): return lax.ppermute(block, axis, route)  62.8 us
    dot_general x4, matrix products, gradient_step(): jnp.einsum('kij,kjn->in', first, right, preferred_element_type=jnp.float32)  51.7 us
    another operation x5, other arithmetic, truncate(): lax.linalg.triangular_solve(factor, sketch.T, left_side=True, lower=True)  39.4 us
  transfers between devices with their start and end apart: 15, of which 15 were waited for; matrix products, arithmetic and copies ran while one was open for 0% of the time, Pallas kernels for 0%

profile of v1, /device:TPU:0, one launch (start us, length us, event | category | flops | bytes accessed | tf_op | source)
XLA Modules:
  0.0 914.0 jit_solution(1305911314158565149)
XLA Ops:
  6.5 5.0 collective-permute-start
  11.5 22.6 %collective-permute-done = bf16[512,1024]{1,0:T(8,128)(2,1)S(1)} collective-permute-done((bf16[512,1024]{1,0:T(8,128)(2,1)}, bf16[512,1024]{1,0:T(8,128)(2,1)S(1)}, u32[]{:S(2)}, u32[]{:S(2)}) %collective-permute-start) | collective-permute-done | bytes 1048608 | tf_op jit(solution)/shard_map/ppermute | solution.py:27
  34.2 1.6 add_convert_fusion.1
  35.8 1.6 collective-permute-start.1
  37.3 22.5 %collective-permute-done.1 = bf16[512,1024]{1,0:T(8,128)(2,1)S(1)} collective-permute-done((bf16[512,1024]{1,0:T(8,128)(2,1)S(1)}, bf16[512,1024]{1,0:T(8,128)(2,1)S(1)}, u32[]{:S(2)}, u32[]{:S(2)}) %collective-permute-start.1) | collective-permute-done | bytes 1048608 | tf_op jit(solution)/shard_map/ppermute | solution.py:17
  59.8 12.3 %fusion.82 = f32[512,1024]{1,0:T(8,128)} fusion(bf16[1,3,1024,1024]{3,2,1,0:T(8,128)(2,1)} %param.15, bf16[1,3,512,1024]{3,2,1,0:T(8,128)(2,1)} %param.14, s32[]{:T(128)S(6)} %select_n.23, bf16[512,1024]{1,0:T(8,128)(2,1)S(1)} %add_convert_fusion.1, bf16[512,1024]{1,0:T(8,128)(2,1)S(1)} %collective-permute-done.1), kind=kOutput, calls=%fused_computation.88 | convolution fusion | flops 6452412416 | bytes 13631492 | tf_op jit(solution)/shard_map/kij,kjn->in/dot_general | solution.py:39
  72.3 53.5 %all-reduce.10.cloned.1.call-done = f32[512,1024]{1,0:T(8,128)} async-done(((f32[512,1024]{1,0:T(8,128)}), f32[512,1024]{1,0:T(8,128)}) %all-reduce.10.cloned.1.call-update) | async-done | bytes 2097168 | tf_op jit(solution)/shard_map/psum | solution.py:40
  125.8 2.7 multiply_reduce_fusion.3
  128.5 5.7 psum.85
  134.9 2.0 multiply_convert_fusion.4
  136.9 1.5 collective-permute-start.2
  138.5 22.2 %collective-permute-done.2 = bf16[512,1024]{1,0:T(8,128)(2,1)S(1)} collective-permute-done((bf16[512,1024]{1,0:T(8,128)(2,1)S(1)}, bf16[512,1024]{1,0:T(8,128)(2,1)S(1)}, u32[]{:S(2)}, u32[]{:S(2)}) %collective-permute-start.2) | collective-permute-done | bytes 1048608 | tf_op jit(solution)/shard_map/ppermute | solution.py:17
  160.7 12.3 %fusion.91 = f32[512,1024]{1,0:T(8,128)} fusion(bf16[1,3,1024,1024]{3,2,1,0:T(8,128)(2,1)} %param.15, bf16[1,3,512,1024]{3,2,1,0:T(8,128)(2,1)} %param.14, s32[]{:T(128)S(6)} %select_n.23, bf16[512,1024]{1,0:T(8,128)(2,1)S(1)} %multiply_convert_fusion.4, bf16[512,1024]{1,0:T(8,128)(2,1)S(1)} %collective-permute-done.2), kind=kOutput, calls=%fused_computation.89 | convolution fusion | flops 6452412416 | bytes 13631492 | tf_op jit(solution)/shard_map/kij,kjn->in/dot_general | solution.py:39
  173.1 51.7 %all-reduce.12.cloned.1.call-done = f32[512,1024]{1,0:T(8,128)} async-done(((f32[512,1024]{1,0:T(8,128)}), f32[512,1024]{1,0:T(8,128)}) %all-reduce.12.cloned.1.call-update) | async-done | bytes 2097168 | tf_op jit(solution)/shard_map/psum | solution.py:40
  224.8 2.8 multiply_reduce_fusion.2
  227.6 5.5 psum.87
  233.8 2.2 multiply_convert_fusion.3
  236.4 2.0 fusion.189
  238.5 1.7 fusion.188
  241.1 45.2 %all-reduce.20.cloned.1.call-done = (f32[256,1024]{1,0:T(8,128)}, f32[256,256]{0,1:T(8,128)}) async-done(((f32[256,1024]{1,0:T(8,128)}, f32[256,256]{0,1:T(8,128)}), (f32[256,1024]{1,0:T(8,128)}, f32[256,256]{0,1:T(8,128)})) %all-reduce.20.cloned.1.call-update) | async-done | bytes 1310736 | tf_op jit(solution)/shard_map/psum | solution.py:61
  286.4 1.2 copy.8
  288.6 11.7 %cholesky.130 = f32[128,128]{1,0:T(8,128)S(1)} custom-call(f32[128,128]{1,0:T(8,128)S(1)} %cholesky.194), custom_call_target="Cholesky" | custom-call | tf_op jit(solution)/shard_map/jit(cholesky)/cholesky | solution.py:68
  300.3 9.8 %custom-call.17 = f32[1,128,128]{1,2,0:T(8,128)S(1)} custom-call(f32[1,128,128]{2,1,0:T(8,128)S(1)} %get-tuple-element.72), custom_call_target="InvertDiagBlocksLowerTriangular" | custom-call | tf_op jit(solution)/shard_map/jit(cholesky)/cholesky | solution.py:68
  310.6 11.7 %cholesky.147 = f32[128,128]{1,0:T(8,128)S(1)} custom-call(f32[128,128]{1,0:T(8,128)S(1)} %convolution_subtract_fusion.5), custom_call_target="Cholesky" | custom-call | tf_op jit(solution)/shard_map/jit(cholesky)/cholesky | solution.py:68
  324.6 4.6 while.8
  325.6 1.4 bitcast_dynamic-update-slice_fusion.4
  327.7 1.4 bitcast_dynamic-update-slice_fusion.4
  329.1 19.7 %custom-call.18 = f32[2,128,128]{1,2,0:T(8,128)S(1)} custom-call(f32[2,128,128]{2,1,0:T(8,128)S(1)} %get-tuple-element.37), custom_call_target="InvertDiagBlocksLowerTriangular" | custom-call | tf_op jit(solution)/shard_map/triangular_solve/custom-call.0 | solution.py:70
  352.2 2.0 convolution_convert_fusion.1
  354.6 24.6 %collective-permute-done.4 = bf16[512,1024]{1,0:T(8,128)(2,1)S(1)} collective-permute-done((bf16[512,1024]{1,0:T(8,128)(2,1)S(1)}, bf16[512,1024]{1,0:T(8,128)(2,1)S(1)}, u32[]{:S(2)}, u32[]{:S(2)}) %collective-permute-start.4) | collective-permute-done | bytes 1048608 | tf_op jit(solution)/shard_map/ppermute | solution.py:17
  379.2 4.9 fusion.13
  384.0 6.4 fusion.9
  390.7 144.4 %reduce-scatter.2.cloned.1.call-done = f32[512,3,1024]{2,0,1:T(8,128)} async-done(((f32[1024,3,1024]{2,0,1:T(8,128)}), f32[512,3,1024]{2,0,1:T(8,128)}) %reduce-scatter.2.cloned.1.call-update) | async-done | bytes 6291472 | tf_op jit(solution)/shard_map/reduce_scatter | solution.py:90
  535.1 3.7 multiply_convert_fusion
  538.8 5.1 collective-permute-start.5
  543.9 1.3 collective-permute-start.3
  545.2 25.2 %collective-permute-done.3 = bf16[512,1024]{1,0:T(8,128)(2,1)S(1)} collective-permute-done((bf16[512,1024]{1,0:T(8,128)(2,1)S(1)}, bf16[512,1024]{1,0:T(8,128)(2,1)S(1)}, u32[]{:S(2)}, u32[]{:S(2)}) %collective-permute-start.3) | collective-permute-done | bytes 1048608 | tf_op jit(solution)/shard_map/ppermute | solution.py:27
  571.4 23.1 %collective-permute-done.6 = bf16[512,1024]{1,0:T(8,128)(2,1)S(1)} collective-permute-done((bf16[512,1024]{1,0:T(8,128)(2,1)S(1)}, bf16[512,1024]{1,0:T(8,128)(2,1)S(1)}, u32[]{:S(2)}, u32[]{:S(2)}) %collective-permute-start.6) | collective-permute-done | bytes 1048608 | tf_op jit(solution)/shard_map/ppermute | solution.py:17
  594.6 15.0 %collective-permute-done.5 = bf16[512,3,1024]{2,0,1:T(8,128)(2,1)} collective-permute-done((bf16[512,3,1024]{2,0,1:T(8,128)(2,1)S(1)}, bf16[512,3,1024]{2,0,1:T(8,128)(2,1)}, u32[]{:S(2)}, u32[]{:S(2)}) %collective-permute-start.5) | collective-permute-done | bytes 3145760 | tf_op jit(solution)/shard_map/ppermute | solution.py:27
  609.6 13.6 %fusion.100 = f32[512,1024]{1,0:T(8,128)} fusion(bf16[1,3,1024,1024]{3,2,1,0:T(8,128)(2,1)} %param.15, s32[]{:T(128)S(6)} %select_n.23, bf16[512,1024]{1,0:T(8,128)(2,1)S(1)} %add_convert_fusion, bf16[512,1024]{1,0:T(8,128)(2,1)S(1)} %collective-permute-done.6, bf16[512,3,1024]{2,0,1:T(8,128)(2,1)} %collective-permute-done.5, ...), kind=kOutput, calls=%fused_computation.90 | convolution fusion | flops 6458703872 | bytes 16777220 | tf_op jit(solution)/shard_map/kij,kjn->in/dot_general | solution.py:39
  623.2 52.6 %all-reduce.14.cloned.1.call-done = f32[512,1024]{1,0:T(8,128)} async-done(((f32[512,1024]{1,0:T(8,128)}), f32[512,1024]{1,0:T(8,128)}) %all-reduce.14.cloned.1.call-update) | async-done | bytes 2097168 | tf_op jit(solution)/shard_map/psum | solution.py:40
  675.8 2.7 multiply_reduce_fusion.1
  678.6 5.5 psum.91
  684.8 2.0 multiply_convert_fusion.2
  686.8 1.5 collective-permute-start.7
  688.3 22.3 %collective-permute-done.7 = bf16[512,1024]{1,0:T(8,128)(2,1)} collective-permute-done((bf16[512,1024]{1,0:T(8,128)(2,1)S(1)}, bf16[512,1024]{1,0:T(8,128)(2,1)}, u32[]{:S(2)}, u32[]{:S(2)}) %collective-permute-start.7) | collective-permute-done | bytes 1048608 | tf_op jit(solution)/shard_map/ppermute | solution.py:17
  710.6 13.4 %fusion.107 = f32[512,1024]{1,0:T(8,128)} fusion(bf16[1,3,1024,1024]{3,2,1,0:T(8,128)(2,1)} %param.15, s32[]{:T(128)S(6)} %select_n.23, bf16[512,1024]{1,0:T(8,128)(2,1)S(1)} %multiply_convert_fusion.2, bf16[512,1024]{1,0:T(8,128)(2,1)} %collective-permute-done.7, bf16[512,3,1024]{2,0,1:T(8,128)(2,1)} %collective-permute-done.5, ...), kind=kOutput, calls=%fused_computation.91 | convolution fusion | flops 6458703872 | bytes 16777220 | tf_op jit(solution)/shard_map/kij,kjn->in/dot_general | solution.py:39
  724.1 51.7 %all-reduce.16.cloned.1.call-done = f32[512,1024]{1,0:T(8,128)} async-done(((f32[512,1024]{1,0:T(8,128)}), f32[512,1024]{1,0:T(8,128)}) %all-reduce.16.cloned.1.call-update) | async-done | bytes 2097168 | tf_op jit(solution)/shard_map/psum | solution.py:40
  775.9 2.8 multiply_reduce_fusion
  778.6 5.8 psum.93
  785.1 2.2 multiply_convert_fusion.1
  787.7 2.0 fusion.191
  789.7 1.7 fusion.190
  791.5 46.2 %all-reduce.18.cloned.1.call-done = (f32[256,1024]{1,0:T(8,128)}, f32[256,256]{0,1:T(8,128)}) async-done(((f32[256,1024]{1,0:T(8,128)}, f32[256,256]{0,1:T(8,128)}), (f32[256,1024]{1,0:T(8,128)}, f32[256,256]{0,1:T(8,128)})) %all-reduce.18.cloned.1.call-update) | async-done | bytes 1310736 | tf_op jit(solution)/shard_map/psum | solution.py:61
  837.6 1.2 copy.11
  838.8 1.0 fusion.144
  839.8 11.7 %cholesky.164 = f32[128,128]{1,0:T(8,128)S(1)} custom-call(f32[128,128]{1,0:T(8,128)S(1)} %cholesky.197), custom_call_target="Cholesky" | custom-call | tf_op jit(solution)/shard_map/jit(cholesky)/cholesky | solution.py:68
  851.6 9.8 %custom-call.20 = f32[1,128,128]{1,2,0:T(8,128)S(1)} custom-call(f32[1,128,128]{2,1,0:T(8,128)S(1)} %get-tuple-element.68), custom_call_target="InvertDiagBlocksLowerTriangular" | custom-call | tf_op jit(solution)/shard_map/jit(cholesky)/cholesky | solution.py:68
  861.9 12.0 %cholesky.181 = f32[128,128]{1,0:T(8,128)S(1)} custom-call(f32[128,128]{1,0:T(8,128)S(1)} %convolution_subtract_fusion.4), custom_call_target="Cholesky" | custom-call | tf_op jit(solution)/shard_map/jit(cholesky)/cholesky | solution.py:68
  876.6 4.1 while.9
  877.2 1.4 bitcast_dynamic-update-slice_fusion.5
  879.3 1.4 bitcast_dynamic-update-slice_fusion.5
  880.7 19.7 %custom-call.21 = f32[2,128,128]{1,2,0:T(8,128)S(1)} custom-call(f32[2,128,128]{2,1,0:T(8,128)S(1)} %get-tuple-element.39), custom_call_target="InvertDiagBlocksLowerTriangular" | custom-call | tf_op jit(solution)/shard_map/triangular_solve/custom-call.0 | solution.py:70
  903.7 3.0 fusion.114
  (72 shorter events, 16.4 us)
Async XLA Ops:
  6.5 119.3 %all-reduce.10.cloned.1.call-start = ((), (), s32[]{:S(2)}) async-start(), calls=%async_computation.1 | async-start | bytes 4194304 | tf_op jit(solution)/shard_map/psum | solution.py:40
  6.5 27.6 %collective-permute-start = (bf16[512,1024]{1,0:T(8,128)(2,1)}, bf16[512,1024]{1,0:T(8,128)(2,1)S(1)}, u32[]{:S(2)}, u32[]{:S(2)}) collective-permute-start(bf16[512,1024]{1,0:T(8,128)(2,1)} %bitcast.221), channel_id=1, source_target_pairs={{0,8},{8,16},{16,24},{1,9},{9,17},{17,25},{2,10},{10,18},{18,26},{... | collective-permute-start | bytes 3145736 | tf_op jit(solution)/shard_map/ppermute | solution.py:27
  35.8 24.1 %collective-permute-start.1 = (bf16[512,1024]{1,0:T(8,128)(2,1)S(1)}, bf16[512,1024]{1,0:T(8,128)(2,1)S(1)}, u32[]{:S(2)}, u32[]{:S(2)}) collective-permute-start(bf16[512,1024]{1,0:T(8,128)(2,1)S(1)} %add_convert_fusion.1), channel_id=1, source_target_pairs={{0,1},{1,0},{2,3},{3,2},{4,5},{5,4},{6,7},{7,6},{8,9},{9,8},{10,11... | collective-permute-start | bytes 3145736 | tf_op jit(solution)/shard_map/ppermute | solution.py:17
  72.2 152.6 %all-reduce.12.cloned.1.call-start = ((), (), s32[]{:S(2)}) async-start(), calls=%async_computation.2 | async-start | bytes 4194304 | tf_op jit(solution)/shard_map/psum | solution.py:40
  136.9 23.7 %collective-permute-start.2 = (bf16[512,1024]{1,0:T(8,128)(2,1)S(1)}, bf16[512,1024]{1,0:T(8,128)(2,1)S(1)}, u32[]{:S(2)}, u32[]{:S(2)}) collective-permute-start(bf16[512,1024]{1,0:T(8,128)(2,1)S(1)} %multiply_convert_fusion.4), channel_id=1, source_target_pairs={{0,1},{1,0},{2,3},{3,2},{4,5},{5,4},{6,7},{7,6},{8,9},{9,8},{10,11... | collective-permute-start | bytes 3145736 | tf_op jit(solution)/shard_map/ppermute | solution.py:17
  173.0 113.3 %all-reduce.20.cloned.1.call-start = ((), (), s32[]{:S(2)}) async-start(), calls=%async_computation.7 | async-start | bytes 2621440 | tf_op jit(solution)/shard_map/psum | solution.py:61
  227.6 8.4 copy-start.4
  240.2 295.0 %reduce-scatter.2.cloned.1.call-start = ((), (), s32[]{:S(2)}) async-start(), calls=%async_computation.3 | async-start | bytes 18874368 | tf_op jit(solution)/shard_map/reduce_scatter | solution.py:90
  286.4 63.9 %copy-start = (f32[256,1024]{1,0:T(8,128)S(1)}, f32[256,1024]{1,0:T(8,128)}, u32[]{:S(2)}) copy-start(f32[256,1024]{1,0:T(8,128)} %get-tuple-element.59) | copy-start | bytes 3145732
  350.3 28.9 %copy-start.3 = (bf16[1,3,512,1024]{3,2,1,0:T(8,128)(2,1)S(1)}, bf16[1,3,512,1024]{3,2,1,0:T(8,128)(2,1)}, u32[]{:S(2)}) copy-start(bf16[1,3,512,1024]{3,2,1,0:T(8,128)(2,1)} %param.14) | copy-start | bytes 9437188
  354.2 25.0 %collective-permute-start.4 = (bf16[512,1024]{1,0:T(8,128)(2,1)S(1)}, bf16[512,1024]{1,0:T(8,128)(2,1)S(1)}, u32[]{:S(2)}, u32[]{:S(2)}) collective-permute-start(bf16[512,1024]{1,0:T(8,128)(2,1)S(1)} %convolution_convert_fusion.1), channel_id=1, source_target_pairs={{0,1},{1,0},{2,3},{3,2},{4,5},{5,4},{6,7},{7,6},{8,9},{9,8},{10,11... | collective-permute-start | bytes 3145736 | tf_op jit(solution)/shard_map/ppermute | solution.py:17
  390.5 179.9 %copy-start.2 = (f32[1,1024]{1,0:T(1,128)S(1)}, f32[1,1024]{1,0:T(1,128)}, u32[]{:S(2)}) copy-start(f32[1,1024]{1,0:T(1,128)} %param.16) | copy-start | bytes 12292
  390.5 285.3 %all-reduce.14.cloned.1.call-start = ((), (), s32[]{:S(2)}) async-start(), calls=%async_computation.4 | async-start | bytes 4194304 | tf_op jit(solution)/shard_map/psum | solution.py:40
  538.8 70.7 %collective-permute-start.5 = (bf16[512,3,1024]{2,0,1:T(8,128)(2,1)S(1)}, bf16[512,3,1024]{2,0,1:T(8,128)(2,1)}, u32[]{:S(2)}, u32[]{:S(2)}) collective-permute-start(bf16[512,3,1024]{2,0,1:T(8,128)(2,1)S(1)} %multiply_convert_fusion), channel_id=1, source_target_pairs={{0,8},{8,16},{16,24},{1,9},{9,17},{17,25},{2,10},{10,18},{18,26},{... | collective-permute-start | bytes 9437192 | tf_op jit(solution)/shard_map/ppermute | solution.py:27
  543.9 26.5 %collective-permute-start.3 = (bf16[512,1024]{1,0:T(8,128)(2,1)S(1)}, bf16[512,1024]{1,0:T(8,128)(2,1)S(1)}, u32[]{:S(2)}, u32[]{:S(2)}) collective-permute-start(bf16[512,1024]{1,0:T(8,128)(2,1)S(1)} %convolution_convert_fusion.1), channel_id=1, source_target_pairs={{8,0},{16,8},{24,16},{9,1},{17,9},{25,17},{10,2},{18,10},{26,18},{... | collective-permute-start | bytes 3145736 | tf_op jit(solution)/shard_map/ppermute | solution.py:27
  570.8 23.7 %collective-permute-start.6 = (bf16[512,1024]{1,0:T(8,128)(2,1)S(1)}, bf16[512,1024]{1,0:T(8,128)(2,1)S(1)}, u32[]{:S(2)}, u32[]{:S(2)}) collective-permute-start(bf16[512,1024]{1,0:T(8,128)(2,1)S(1)} %add_convert_fusion), channel_id=1, source_target_pairs={{0,1},{1,0},{2,3},{3,2},{4,5},{5,4},{6,7},{7,6},{8,9},{9,8},{10,11... | collective-permute-start | bytes 3145736 | tf_op jit(solution)/shard_map/ppermute | solution.py:17
  623.2 152.7 %all-reduce.16.cloned.1.call-start = ((), (), s32[]{:S(2)}) async-start(), calls=%async_computation.5 | async-start | bytes 4194304 | tf_op jit(solution)/shard_map/psum | solution.py:40
  686.8 23.8 %collective-permute-start.7 = (bf16[512,1024]{1,0:T(8,128)(2,1)S(1)}, bf16[512,1024]{1,0:T(8,128)(2,1)}, u32[]{:S(2)}, u32[]{:S(2)}) collective-permute-start(bf16[512,1024]{1,0:T(8,128)(2,1)S(1)} %multiply_convert_fusion.2), channel_id=1, source_target_pairs={{0,1},{1,0},{2,3},{3,2},{4,5},{5,4},{6,7},{7,6},{8,9},{9,8},{10,11... | collective-permute-start | bytes 3145736 | tf_op jit(solution)/shard_map/ppermute | solution.py:17
  724.1 113.5 %all-reduce.18.cloned.1.call-start = ((), (), s32[]{:S(2)}) async-start(), calls=%async_computation.6 | async-start | bytes 2621440 | tf_op jit(solution)/shard_map/psum | solution.py:61
  837.6 64.2 %copy-start.1 = (f32[256,1024]{1,0:T(8,128)S(1)}, f32[256,1024]{1,0:T(8,128)}, u32[]{:S(2)}) copy-start(f32[256,1024]{1,0:T(8,128)} %get-tuple-element.57) | copy-start | bytes 3145732
Sparse Core Ops, SparseCore 0:
  72.3 53.4 all-reduce.9
  173.2 51.5 all-reduce.11
  240.3 46.0 all-reduce.19
  390.6 144.4 reduce-scatter.1
  623.3 52.4 all-reduce.13
  724.2 51.5 all-reduce.15
  791.6 46.0 all-reduce.17
